TPU v7x, 32 devices: a whole 2x2x4 slice. The times are simulated.
32 devices in a mesh: depth: 2 (over core), dp: 16 (over z, y, x).
Axes of the slice: x: 2, y: 2, z: 4, core: 2. Of those that a mesh axis runs over, the one named last changes fastest.
Arguments:
- inputs: bfloat16 [64, 512, 768], P(('depth', 'dp')), may hold values from -6 to 6
- output_gradient: bfloat16 [64, 512, 768], P(('depth', 'dp')), may hold values from -6 to 6
- keep: int32 [64], P(('depth', 'dp')), may hold values 0 or 1
- lengths: int32 [64], P(('depth', 'dp')), may hold values from 64 to 512
- routes: int32 [64], P(('depth', 'dp')), may hold values from 0 to 1
- attn_weights: float32 [256, 96, 96], P(('depth', 'dp'))
- attn_stats: float32 [256, 2, 96, 96], P(('depth', 'dp'))
- attn_roots: float32 [256, 2, 96, 96], P(('depth', 'dp'))
- attn_momentum: float32 [256, 96, 96], P(('depth', 'dp')), may hold values from -0.005859375 to 0.005859375
- ffn_weights: float32 [512, 96, 96], P(('depth', 'dp'))
- ffn_stats: float32 [512, 2, 96, 96], P(('depth', 'dp'))
- ffn_roots: float32 [512, 2, 96, 96], P(('depth', 'dp'))
- ffn_momentum: float32 [512, 96, 96], P(('depth', 'dp')), may hold values from -0.005859375 to 0.005859375
- vec_weights: float32 [9216], P(('depth', 'dp'))
- vec_first: float32 [9216], P(('depth', 'dp')), may hold values from -0.0012207031 to 0.0012207031
- vec_second: float32 [9216], P(('depth', 'dp')), may hold values from 5.644054e-10 to 2.2576216e-09
Outputs:
- out: bfloat16 [64, 512, 768], P(('depth', 'dp'))
- in_grad: bfloat16 [64, 512, 768], P(('depth', 'dp'))
- grad_norm: float32 [], replicated
- attn_stats_new: float32 [256, 2, 96, 96], P(('depth', 'dp'))
- attn_momentum_new: float32 [256, 96, 96], P(('depth', 'dp'))
- attn_weights_new: float32 [256, 96, 96], P(('depth', 'dp'))
- ffn_stats_new: float32 [512, 2, 96, 96], P(('depth', 'dp'))
- ffn_momentum_new: float32 [512, 96, 96], P(('depth', 'dp'))
- ffn_weights_new: float32 [512, 96, 96], P(('depth', 'dp'))
- vec_first_new: float32 [9216], P(('depth', 'dp'))
- vec_second_new: float32 [9216], P(('depth', 'dp'))
- vec_weights_new: float32 [9216], P(('depth', 'dp'))
All inputs are finite; a program needn't handle non-finite values. No bound on the sum of `keep` on one device may be relied on, other than what follows from the above.
Results may differ from a plain program's by a relative error of at most 0.012.
The roundings to bfloat16 on the way count: a program that leaves them out, or rounds other values in their place, can miss the bound.
Values may be sent and summed in bfloat16 or wider, within the bound.
A program may use at most 192 MiB of HBM per device.

v0:
```python
import math

import jax
import jax.numpy as jnp
from jax import lax
from jax.sharding import PartitionSpec as P

HEADS = 12
FF = 3072
BLOCK = 96
STEP = 10


norm_floor = 1e-05
masked_fill = -1000000000.0
momentum_decay = 0.9
stat_decay = 0.95
matrix_rate = 1.0
matrix_decay = 0.01
clip_bound = 1.0
first_decay = 0.9
second_decay = 0.999
vector_rate = 0.5
adam_floor = 1e-08


def serve_flags(keep_rows, route_rows):
    count = keep_rows.shape[-1]
    order = jnp.arange(count, dtype=jnp.int32)
    earlier = (order[None, :] < order[:, None]).astype(jnp.int32)
    same = (route_rows[:, :, None] == route_rows[:, None, :]).astype(jnp.int32)
    clash = jnp.sum(same * earlier[None, :, :] * keep_rows[:, None, :], axis=2)
    return keep_rows * (clash == 0).astype(jnp.int32)


def to_matrix(blocks, height, breadth):
    shaped = blocks.reshape(height // BLOCK, breadth // BLOCK, BLOCK, BLOCK)
    return shaped.transpose(0, 2, 1, 3).reshape(height, breadth)


def to_flat_blocks(matrix):
    height, breadth = matrix.shape
    shaped = matrix.reshape(height // BLOCK, BLOCK, breadth // BLOCK, BLOCK)
    return shaped.transpose(0, 2, 1, 3).reshape(-1, BLOCK * BLOCK)


def norm_parts(resid):
    center = resid - jnp.mean(resid, axis=-1, keepdims=True)
    factor = lax.rsqrt(jnp.mean(center * center, axis=-1, keepdims=True) + norm_floor)
    return (center * factor, factor)


def norm_back(grad_normed, normed, factor):
    middle = jnp.mean(grad_normed, axis=-1, keepdims=True)
    along = jnp.mean(grad_normed * normed, axis=-1, keepdims=True)
    return factor * (grad_normed - middle - normed * along)


def gelu_slope(value):
    cumulative = 0.5 * (1.0 + lax.erf(value * (1.0 / math.sqrt(2.0))))
    density = jnp.exp(-0.5 * value * value) * (1.0 / math.sqrt(2.0 * math.pi))
    return cumulative + value * density


def product(left, right):
    return jnp.dot(left, right, preferred_element_type=jnp.float32)


def contract_rows(left, right):
    return lax.dot_general(
        left, right, (((0,), (0,)), ((), ())), preferred_element_type=jnp.float32
    )


def times_transpose(left, right):
    return lax.dot_general(
        left, right, (((1,), (1,)), ((), ())), preferred_element_type=jnp.float32
    )


def masked_scores(query, keys, visible_len):
    scale = 1.0 / math.sqrt(query.shape[-1])
    scores = jnp.einsum("qhe,khe->hqk", query, keys, preferred_element_type=jnp.float32) * scale
    visible = jnp.arange(keys.shape[0], dtype=jnp.int32) < visible_len
    return jnp.where(visible[None, None, :], scores, masked_fill)


def attend_forward(pieces):
    query, keys, values, visible_len = pieces
    scores = masked_scores(query, keys, visible_len)
    peak = jnp.max(scores, axis=-1, keepdims=True)
    expo = jnp.exp(scores - peak)
    total = jnp.sum(expo, axis=-1, keepdims=True)
    probs_low = (expo / total).astype(jnp.bfloat16)
    context = jnp.einsum("hqk,khe->qhe", probs_low, values, preferred_element_type=jnp.float32)
    return (context, peak[..., 0] + jnp.log(total[..., 0]))


def attend_backward(pieces):
    query, keys, values, grad_ctx, log_total, visible_len = pieces
    scale = 1.0 / math.sqrt(query.shape[-1])
    scores = masked_scores(query, keys, visible_len)
    probs = jnp.exp(scores - log_total[..., None])
    probs_low = probs.astype(jnp.bfloat16)
    grad_probs = jnp.einsum("qhe,khe->hqk", grad_ctx, values, preferred_element_type=jnp.float32)
    grad_values = jnp.einsum(
        "hqk,qhe->khe", probs_low, grad_ctx, preferred_element_type=jnp.float32
    )
    along = jnp.sum(probs * grad_probs, axis=-1, keepdims=True)
    grad_scores = (probs * (grad_probs - along)).astype(jnp.bfloat16)
    grad_query = (
        jnp.einsum("hqk,khe->qhe", grad_scores, keys, preferred_element_type=jnp.float32) * scale
    )
    grad_keys = (
        jnp.einsum("hqk,qhe->khe", grad_scores, query, preferred_element_type=jnp.float32) * scale
    )
    return (grad_query, grad_keys, grad_values)


def shampoo(weights, stats, roots, momentum, grads, factor):
    highest = lax.Precision.HIGHEST
    clipped = grads * factor
    moment = momentum_decay * momentum + clipped
    left = jnp.einsum("nab,ncb->nac", clipped, clipped, precision=highest)
    right = jnp.einsum("nab,nac->nbc", clipped, clipped, precision=highest)
    fresh = stat_decay * stats + (1.0 - stat_decay) * jnp.stack([left, right], axis=1)
    turned = jnp.einsum("nab,nbc->nac", roots[:, 0], moment, precision=highest)
    turned = jnp.einsum("nab,nbc->nac", turned, roots[:, 1], precision=highest)
    updated = weights - matrix_rate * (turned + matrix_decay * weights)
    return (fresh, moment, updated)


def adam_step(weights, first, second, grads, factor):
    clipped = grads * factor
    first_new = first_decay * first + (1.0 - first_decay) * clipped
    second_new = second_decay * second + (1.0 - second_decay) * clipped * clipped
    first_hat = first_new / (1.0 - first_decay**STEP)
    second_hat = second_new / (1.0 - second_decay**STEP)
    updated = weights - vector_rate * first_hat / (jnp.sqrt(second_hat) + adam_floor)
    return (first_new, second_new, updated)


def per_device(
    inputs,
    output_gradient,
    keep,
    lengths,
    routes,
    attn_weights,
    attn_stats,
    attn_roots,
    attn_momentum,
    ffn_weights,
    ffn_stats,
    ffn_roots,
    ffn_momentum,
    vec_weights,
    vec_first,
    vec_second,
):
    slots, seq_len, width = inputs.shape
    tokens = slots * seq_len
    head_size = width // HEADS
    hidden_width = FF
    depth_count = lax.axis_size("depth")
    peer_slots = slots // depth_count
    grid = (width // BLOCK) ** 2
    half_ffn = width * hidden_width // (BLOCK * BLOCK)
    area = BLOCK * BLOCK
    low_type = jnp.bfloat16
    attn_flat = attn_weights.reshape(-1, area).astype(low_type)
    ffn_flat = ffn_weights.reshape(-1, area).astype(low_type)
    attn_all, ffn_all, vec_all = (
        lax.all_gather(attn_flat, ("depth", "dp"), axis=0, tiled=True),
        lax.all_gather(ffn_flat, ("depth", "dp"), axis=0, tiled=True),
        lax.all_gather(vec_weights.astype(low_type), ("depth", "dp"), axis=0, tiled=True),
    )
    table_keep, table_len, table_route = (
        lax.all_gather(keep, "depth", axis=0, tiled=True),
        lax.all_gather(lengths, "depth", axis=0, tiled=True),
        lax.all_gather(routes, "depth", axis=0, tiled=True),
    )
    mine = serve_flags(keep[None, :], routes[None, :])[0]
    slot_order = jnp.arange(slots, dtype=jnp.int32)
    selection = ((routes[None, :] == slot_order[:, None]).astype(jnp.int32) * mine[None, :]).astype(
        low_type
    )
    outgoing_rows = jnp.einsum(
        "gz,zrp->grp", selection, inputs, preferred_element_type=jnp.float32
    ).astype(low_type)
    send_grad = jnp.einsum(
        "gz,zrp->grp", selection, output_gradient, preferred_element_type=jnp.float32
    ).astype(low_type)
    come_rows, come_grad = (
        lax.all_to_all(outgoing_rows, "depth", split_axis=0, concat_axis=0, tiled=True),
        lax.all_to_all(send_grad, "depth", split_axis=0, concat_axis=0, tiled=True),
    )
    all_keep = table_keep.reshape(depth_count, slots)
    all_route = table_route.reshape(depth_count, slots)
    all_len = table_len.reshape(depth_count, slots)
    all_served = serve_flags(all_keep, all_route)
    here = lax.axis_index("depth")
    source = slot_order // peer_slots
    target = here * peer_slots + slot_order % peer_slots
    source_hot = (source[:, None] == jnp.arange(depth_count, dtype=jnp.int32)[None, :]).astype(
        jnp.int32
    )
    match = (all_route[None, :, :] == target[:, None, None]).astype(jnp.int32) * all_served[
        None, :, :
    ]
    slot_len = jnp.sum(source_hot[:, :, None] * match * all_len[None, :, :], axis=(1, 2))
    visible_len = jnp.maximum(slot_len, 1)
    query_w = to_matrix(attn_all[0:grid], width, width)
    key_w = to_matrix(attn_all[grid : 2 * grid], width, width)
    value_w = to_matrix(attn_all[2 * grid : 3 * grid], width, width)
    output_w = to_matrix(attn_all[3 * grid : 4 * grid], width, width)
    vectors = vec_all.astype(jnp.float32)
    q_bias = vectors[0:width]
    v_bias = vectors[width : 2 * width]
    out_bias = vectors[2 * width : 3 * width]
    hidden_bias = vectors[3 * width : 3 * width + hidden_width]
    ffn_bias = vectors[3 * width + hidden_width : 4 * width + hidden_width]
    gain_one = vectors[4 * width + hidden_width : 5 * width + hidden_width]
    shift_one = vectors[5 * width + hidden_width : 6 * width + hidden_width]
    gain_two = vectors[6 * width + hidden_width : 7 * width + hidden_width]
    shift_two = vectors[7 * width + hidden_width : 8 * width + hidden_width]
    flat = come_rows.reshape(tokens, width)
    four = (slots, seq_len, HEADS, head_size)
    query = (product(flat, query_w) + q_bias).astype(low_type).reshape(four)
    keys = product(flat, key_w).astype(low_type).reshape(four)
    values = (product(flat, value_w) + v_bias).astype(low_type).reshape(four)
    context, log_total = lax.map(attend_forward, (query, keys, values, visible_len))
    context_low = context.reshape(tokens, width).astype(low_type)
    attended = product(context_low, output_w) + out_bias
    normed_one, factor_one = norm_parts(flat.astype(jnp.float32) + attended)
    hidden_in = normed_one * gain_one + shift_one
    hidden_low = hidden_in.astype(low_type)
    hidden_w = to_matrix(ffn_all[0:half_ffn], width, hidden_width)
    return_weight = to_matrix(ffn_all[half_ffn:], hidden_width, width)
    before = product(hidden_low, hidden_w) + hidden_bias
    active_low = jax.nn.gelu(before, approximate=False).astype(low_type)
    branch = product(active_low, return_weight) + ffn_bias
    normed_two, factor_two = norm_parts(hidden_in + branch)
    result_low = (normed_two * gain_two + shift_two).astype(low_type)
    grad_rows = come_grad.reshape(tokens, width).astype(jnp.float32)
    grad_gain_two = jnp.sum(grad_rows * normed_two, axis=0)
    grad_shift_two = jnp.sum(grad_rows, axis=0)
    grad_resid_two = norm_back(grad_rows * gain_two, normed_two, factor_two)
    grad_branch = grad_resid_two.astype(low_type)
    grad_ffn_bias = jnp.sum(grad_branch.astype(jnp.float32), axis=0)
    gradient_return_weight = contract_rows(active_low, grad_branch)
    grad_active = times_transpose(grad_branch, return_weight)
    grad_before = (grad_active * gelu_slope(before)).astype(low_type)
    grad_hidden_bias = jnp.sum(grad_before.astype(jnp.float32), axis=0)
    grad_hidden_w = contract_rows(hidden_low, grad_before)
    grad_hidden = times_transpose(grad_before, hidden_w) + grad_resid_two
    grad_gain_one = jnp.sum(grad_hidden * normed_one, axis=0)
    grad_shift_one = jnp.sum(grad_hidden, axis=0)
    grad_resid_one = norm_back(grad_hidden * gain_one, normed_one, factor_one)
    ffn_grad = jnp.concatenate(
        [to_flat_blocks(grad_hidden_w), to_flat_blocks(gradient_return_weight)], axis=0
    )
    grad_attended = grad_resid_one.astype(low_type)
    grad_out_bias = jnp.sum(grad_attended.astype(jnp.float32), axis=0)
    grad_output_w = contract_rows(context_low, grad_attended)
    grad_context = times_transpose(grad_attended, output_w).astype(low_type).reshape(four)
    grad_query, grad_keys, grad_values = lax.map(
        attend_backward, (query, keys, values, grad_context, log_total, visible_len)
    )
    grad_query = grad_query.reshape(tokens, width).astype(low_type)
    grad_keys = grad_keys.reshape(tokens, width).astype(low_type)
    grad_values = grad_values.reshape(tokens, width).astype(low_type)
    grad_q_bias = jnp.sum(grad_query.astype(jnp.float32), axis=0)
    grad_v_bias = jnp.sum(grad_values.astype(jnp.float32), axis=0)
    grad_query_w = contract_rows(flat, grad_query)
    grad_key_w = contract_rows(flat, grad_keys)
    grad_value_w = contract_rows(flat, grad_values)
    in_rows = (
        grad_resid_one
        + times_transpose(grad_query, query_w)
        + times_transpose(grad_keys, key_w)
        + times_transpose(grad_values, value_w)
    )
    attn_grad = jnp.concatenate(
        [
            to_flat_blocks(grad_query_w),
            to_flat_blocks(grad_key_w),
            to_flat_blocks(grad_value_w),
            to_flat_blocks(grad_output_w),
        ],
        axis=0,
    )
    vec_grad = jnp.concatenate(
        [
            grad_q_bias,
            grad_v_bias,
            grad_out_bias,
            grad_hidden_bias,
            grad_ffn_bias,
            grad_gain_one,
            grad_shift_one,
            grad_gain_two,
            grad_shift_two,
        ]
    )
    attn_share, ffn_share, vec_share = (
        lax.psum_scatter(attn_grad, ("depth", "dp"), scatter_dimension=0, tiled=True),
        lax.psum_scatter(ffn_grad, ("depth", "dp"), scatter_dimension=0, tiled=True),
        lax.psum_scatter(vec_grad, ("depth", "dp"), scatter_dimension=0, tiled=True),
    )
    returned_rows, returned_gradient = (
        lax.all_to_all(
            result_low.reshape(slots, seq_len, width),
            "depth",
            split_axis=0,
            concat_axis=0,
            tiled=True,
        ),
        lax.all_to_all(
            in_rows.astype(low_type).reshape(slots, seq_len, width),
            "depth",
            split_axis=0,
            concat_axis=0,
            tiled=True,
        ),
    )
    stay = (1 - mine).astype(jnp.float32)[:, None, None]
    out = (
        jnp.einsum("rx,rmp->xmp", selection, returned_rows, preferred_element_type=jnp.float32)
        + stay * inputs.astype(jnp.float32)
    ).astype(low_type)
    in_grad = (
        jnp.einsum("rx,rmp->xmp", selection, returned_gradient, preferred_element_type=jnp.float32)
        + stay * output_gradient.astype(jnp.float32)
    ).astype(low_type)
    square = (
        jnp.sum(attn_share * attn_share)
        + jnp.sum(ffn_share * ffn_share)
        + jnp.sum(vec_share * vec_share)
    )
    total = lax.psum(square, ("depth", "dp"))
    grad_norm = jnp.sqrt(total)
    factor = clip_bound / jnp.maximum(grad_norm, clip_bound)
    attn_square = attn_share.reshape(-1, BLOCK, BLOCK)
    ffn_square = ffn_share.reshape(-1, BLOCK, BLOCK)
    attn_fresh, attn_moment, attn_updated = shampoo(
        attn_weights, attn_stats, attn_roots, attn_momentum, attn_square, factor
    )
    ffn_fresh, ffn_moment, ffn_updated = shampoo(
        ffn_weights, ffn_stats, ffn_roots, ffn_momentum, ffn_square, factor
    )
    first_new, second_new, vec_updated = adam_step(
        vec_weights, vec_first, vec_second, vec_share, factor
    )
    return (
        out,
        in_grad,
        grad_norm,
        attn_fresh,
        attn_moment,
        attn_updated,
        ffn_fresh,
        ffn_moment,
        ffn_updated,
        first_new,
        second_new,
        vec_updated,
    )


def solution(mesh):
    return jax.shard_map(
        per_device,
        mesh=mesh,
        in_specs=(
            P(("depth", "dp"), None, None),
            P(("depth", "dp"), None, None),
            P(("depth", "dp")),
            P(("depth", "dp")),
            P(("depth", "dp")),
            P(("depth", "dp"), None, None),
            P(("depth", "dp"), None, None, None),
            P(("depth", "dp"), None, None, None),
            P(("depth", "dp"), None, None),
            P(("depth", "dp"), None, None),
            P(("depth", "dp"), None, None, None),
            P(("depth", "dp"), None, None, None),
            P(("depth", "dp"), None, None),
            P(("depth", "dp")),
            P(("depth", "dp")),
            P(("depth", "dp")),
        ),
        out_specs=(
            P(("depth", "dp"), None, None),
            P(("depth", "dp"), None, None),
            P(),
            P(("depth", "dp"), None, None, None),
            P(("depth", "dp"), None, None),
            P(("depth", "dp"), None, None),
            P(("depth", "dp"), None, None, None),
            P(("depth", "dp"), None, None),
            P(("depth", "dp"), None, None),
            P(("depth", "dp")),
            P(("depth", "dp")),
            P(("depth", "dp")),
        ),
        check_vma=False,
    )
```

profile of v0, /device:TPU:0, one launch (start us, length us, event | category | flops | bytes accessed | tf_op | source)
XLA Modules:
  0.0 844.8 jit_solution(4913580645083294062)
XLA Ops:
  27.2 42.8 %all-reduce = bf16[9216]{0:T(1024)(128)(2,1)S(1)} all-reduce(bf16[9216]{0:T(1024)(128)(2,1)S(1)} %dynamic-update-slice), channel_id=1, replica_groups=mesh['depth'=2,'dp'=16] {'depth','dp'}, use_global_device_ids=true, to_apply=%add | all-reduce | flops 9216 | bytes 36864
  140.5 22.7 %while.26 = (s32[]{:T(128)}, bf16[2,512,12,64]{1,3,2,0:T(8,128)(2,1)}, f32[2,12,512]{2,1,0:T(8,128)S(1)}, bf16[2,512,12,64]{1,3,2,0:T(8,128)(2,1)}, s32[2]{0:T(1...) while((s32[]{:T(128)}, ...), condition=%wide.region_6.7_spmd, body=%wide.region_3.6_spmd.sunk | while | flops 843049472 | bytes 48214148 | solution.py:232
  178.8 8.5 %fusion.102 = (bf16[256,9216]{1,0:T(8,128)(2,1)}, bf16[256,9216]{1,0:T(8,128)(2,1)}) fusion(bf16[512,9216]{1,0:T(8,128)(2,1)} %all-gather.5.cloned.1.call-done), kind=kLoop, calls=%fused_computation.208 | loop fusion | bytes 18874368 | tf_op jit(solution)/shard_map/slice | solution.py:239
  187.3 10.0 %reshape.394 = bf16[8,32,96,96]{3,2,1,0:T(8,128)(2,1)} reshape(bf16[256,9216]{1,0:T(8,128)(2,1)} %get-tuple-element.371) | data formatting | bytes 9437184 | tf_op jit(solution)/shard_map/reshape | solution.py:37
  197.3 7.8 copy.347
  205.2 12.1 %reshape.395 = bf16[768,3072]{1,0:T(8,128)(2,1)} reshape(bf16[8,96,32,96]{3,2,1,0:T(8,128)(2,1)} %copy.347) | data formatting | bytes 9437184 | tf_op jit(solution)/shard_map/reshape | solution.py:38
  217.2 10.2 %reshape.396 = bf16[32,8,96,96]{3,2,1,0:T(8,128)(2,1)} reshape(bf16[256,9216]{1,0:T(8,128)(2,1)} %get-tuple-element.370) | data formatting | bytes 9437184 | tf_op jit(solution)/shard_map/reshape | solution.py:37
  227.4 8.4 copy.348
  235.8 10.9 %reshape.397 = bf16[3072,768]{1,0:T(8,128)(2,1)} reshape(bf16[32,96,8,96]{3,2,1,0:T(8,128)(2,1)} %copy.348) | data formatting | bytes 9437184 | tf_op jit(solution)/shard_map/reshape | solution.py:38
  246.6 37.0 %fusion.45 = (bf16[1024,3072]{1,0:T(8,128)(2,1)S(1)}, f32[1024,3072]{1,0:T(8,128)}) fusion(f32[3072]{0:T(1024)S(1)} %copy-done.71, bf16[768,3072]{1,0:T(8,128)(2,1)} %reshape.395, f32[1024,768]{1,0:T(8,128)S(1)} %get-tuple-element.386, f32[768]{0:T(1024)S(1)} %copy-done.62, f32[768]{0:T(1024)S(1)} %copy-done.58, f32[1024]{0:T(1024)S(1)} %add_rsqrt_fusion.1, ...), kind=kOutput, calls=%fused_computation.59 | convolution fusion | flops 5043388416 | bytes 26765312 | tf_op jit(solution)/shard_map/dot_general | solution.py:66
  283.7 5.4 fusion.106
  295.2 13.4 %convert_reduce_fusion = (f32[3072]{0:T(1024)}, bf16[1024,3072]{1,0:T(8,128)(2,1)S(1)}) fusion(f32[1024,3072]{1,0:T(8,128)} %get-tuple-element.388, f32[3072]{0:T(1024)S(1)} %copy-done.71, bf16[3072,768]{1,0:T(8,128)(2,1)S(1)} %copy-done.27, f32[1024,768]{1,0:T(8,128)S(1)} %get-tuple-element.361), kind=kOutput, calls=%fused_computation.68 | convolution fusion | flops 4873516032 | bytes 26763264 | tf_op jit(solution)/shard_map/dot_general | solution.py:76
  308.7 6.5 multiply_reduce_fusion.1
  327.6 51.7 %while.27 = (s32[]{:T(128)}, bf16[2,512,12,64]{1,3,2,0:T(8,128)(2,1)}, bf16[2,512,12,64]{1,3,2,0:T(8,128)(2,1)}, bf16[2,512,12,64]{1,3,2,0:T(8,128)(2,1)}, bf16[...) while((s32[]{:T(128)}, ...), condition=%wide.region_17.18_spmd, body=%wide.region_15.17_spmd.sunk | while | flops 2061232640 | bytes 142540080 | solution.py:267
  330.7 7.3 multiply_reduce_fusion.11
  338.1 7.2 multiply_convert_fusion.2
  356.6 7.3 multiply_reduce_fusion.11
  363.9 7.2 multiply_convert_fusion.2
  422.6 7.3 pad_maximum_fusion.1
  431.8 10.8 %fusion.96 = f32[768,3072]{1,0:T(8,128)} fusion(bf16[1024,3072]{1,0:T(8,128)(2,1)} %copy-done.20, f32[1024,768]{1,0:T(8,128)S(1)} %copy-done.5, f32[768]{0:T(1024)S(1)} %copy-done.63, f32[768]{0:T(1024)S(1)} %copy-done.59, f32[1024]{0:T(1024)S(1)} %copy-done.57, f32[1024]{0:T(1024)S(1)} %copy-done.55), kind=kOutput, calls=%fused_computation.206 | convolution fusion | flops 4835770368 | bytes 18888704 | tf_op jit(solution)/shard_map/dot_general | solution.py:70
  442.7 13.4 %reshape.405 = f32[8,96,32,96]{3,2,1,0:T(8,128)} reshape(f32[768,3072]{1,0:T(8,128)} %fusion.96) | data formatting | bytes 18874368 | tf_op jit(solution)/shard_map/reshape | solution.py:43
  456.1 16.9 %copy.432 = f32[8,96,32,96]{3,1,2,0:T(8,128)} copy(f32[8,96,32,96]{3,2,1,0:T(8,128)} %reshape.405) | data formatting | bytes 18874368 | tf_op jit(solution)/shard_map/reshape | solution.py:43
  473.0 13.2 %reshape.406 = f32[256,9216]{1,0:T(8,128)} reshape(f32[8,32,96,96]{3,2,1,0:T(8,128)} %bitcast.311) | data formatting | bytes 18874368 | tf_op jit(solution)/shard_map/reshape | solution.py:44
  486.2 10.6 %fusion.93 = f32[3072,768]{1,0:T(8,128)} fusion(bf16[1024,3072]{1,0:T(8,128)(2,1)} %copy-done.92, f32[1024,768]{1,0:T(8,128)S(1)} %copy-done.31), kind=kOutput, calls=%fused_computation.203 | convolution fusion | flops 4832624640 | bytes 18874368 | tf_op jit(solution)/shard_map/dot_general | solution.py:70
  496.8 13.9 %reshape.407 = f32[32,96,8,96]{3,2,1,0:T(8,128)} reshape(f32[3072,768]{1,0:T(8,128)} %fusion.93) | data formatting | bytes 18874368 | tf_op jit(solution)/shard_map/reshape | solution.py:43
  510.6 11.5 %copy.431 = f32[32,96,8,96]{3,1,2,0:T(8,128)} copy(f32[32,96,8,96]{3,2,1,0:T(8,128)} %reshape.407) | data formatting | bytes 18874368 | tf_op jit(solution)/shard_map/reshape | solution.py:43
  522.1 12.9 %reshape.408 = f32[256,9216]{1,0:T(8,128)} reshape(f32[32,8,96,96]{3,2,1,0:T(8,128)} %bitcast.312) | data formatting | bytes 18874368 | tf_op jit(solution)/shard_map/reshape | solution.py:44
  535.1 14.4 %pad_maximum_fusion = f32[512,9216]{1,0:T(8,128)} fusion(f32[256,9216]{1,0:T(8,128)} %reshape.408, f32[256,9216]{1,0:T(8,128)} %reshape.406), kind=kLoop, calls=%fused_computation.56 | loop fusion | flops 4718592 | bytes 37748736 | tf_op jit(solution)/shard_map/concatenate | solution.py:260
  559.4 5.3 all_to_all.20
  573.5 41.1 %all-reduce.4 = f32[9216]{0:T(1024)S(1)} all-reduce(f32[9216]{0:T(1024)S(1)} %constant_dynamic-update-slice_fusion), channel_id=4, replica_groups=mesh['depth'=2,'dp'=16] {'depth','dp'}, use_global_device_ids=true, to_apply=%region_31.32.clone | all-reduce | flops 9216 | bytes 73728
  621.8 155.8 %reduce-scatter.5.cloned.1.call-done = f32[16,9216]{1,0:T(8,128)} async-done(((f32[512,9216]{1,0:T(8,128)}), f32[16,9216]{1,0:T(8,128)}) %reduce-scatter.5.cloned.1.call-update) | async-done | bytes 589840 | tf_op jit(solution)/shard_map/reduce_scatter | solution.py:308
  782.8 39.0 %psum.7 = f32[]{:T(128)} all-reduce(f32[]{:T(128)S(6)} %add.202), channel_id=1, replica_groups=mesh['depth'=2,'dp'=16] {'depth','dp'}, use_global_device_ids=true, to_apply=%region_33.34 | all-reduce | flops 1 | bytes 8 | tf_op jit(solution)/shard_map/psum | solution.py:341
  (393 shorter events, 256.2 us)
Async XLA Ops:
  7.2 5.9 copy-start.80
  7.2 6.2 copy-start.81
  7.2 7.1 copy-start.83
  7.2 72.4 %all-gather.3.cloned.1.call-start = ((), (), s32[]{:S(2)}) async-start(), calls=%async_computation.6 | async-start | bytes 4866048 | tf_op jit(solution)/shard_map/all_gather | solution.py:174
  9.3 169.4 %all-gather.5.cloned.1.call-start = ((), (), s32[]{:S(2)}) async-start(), calls=%async_computation.7 | async-start | bytes 9732096 | tf_op jit(solution)/shard_map/all_gather | solution.py:175
  14.3 9.6 %copy-start.87 = (bf16[2,2,1]{1,0,2:T(2,128)(2,1)}, bf16[2,2,1]{1,0,2:T(2,128)(2,1)S(1)}, u32[]{:S(2)}) copy-start(bf16[2,2,1]{1,0,2:T(2,128)(2,1)S(1)} %fusion.91) | copy-start | bytes 28
  16.1 7.8 copy-start.72
  16.1 7.8 copy-start.85
  17.6 53.5 %all-to-all-start.2 = ((bf16[2,512,768]{2,1,0:T(8,128)(2,1)}), bf16[2,512,768]{2,1,0:T(8,128)(2,1)S(1)}, u32[]{:S(2)}, u32[]{:S(2)}) async-start(bf16[2,512,768]{2,1,0:T(8,128)(2,1)} %copy.353), calls=%async_computation.2 | async-start | bytes 3145728 | tf_op jit(solution)/shard_map/all_to_all | solution.py:196
  71.1 8.0 copy-start.60
  71.1 8.0 copy-start.8
  71.2 6.2 all-to-all-start
  74.8 545.3 %reduce-scatter.3.cloned.1.call-start = ((), (), s32[]{:S(2)}) async-start(), calls=%async_computation.8 | async-start | bytes 9732096 | tf_op jit(solution)/shard_map/reduce_scatter | solution.py:307
  77.4 52.1 %copy-start.21 = (bf16[2,512,768]{2,1,0:T(8,128)(2,1)}, bf16[2,512,768]{2,1,0:T(8,128)(2,1)S(1)}, u32[]{:S(2)}) copy-start(bf16[2,512,768]{2,1,0:T(8,128)(2,1)S(1)} %all-to-all-done) | copy-start | bytes 4718596
  178.2 137.0 %copy-start.4 = (f32[1024,768]{1,0:T(8,128)}, f32[1024,768]{1,0:T(8,128)S(1)}, u32[]{:S(2)}) copy-start(f32[1024,768]{1,0:T(8,128)S(1)} %get-tuple-element.386) | copy-start | bytes 9437188
  178.2 137.0 %copy-start.54 = (f32[1024]{0:T(1024)}, f32[1024]{0:T(1024)S(1)}, u32[]{:S(2)}) copy-start(f32[1024]{0:T(1024)S(1)} %broadcast_multiply_fusion.6) | copy-start | bytes 12292
  178.8 136.5 %copy-start.56 = (f32[1024]{0:T(1024)}, f32[1024]{0:T(1024)S(1)}, u32[]{:S(2)}) copy-start(f32[1024]{0:T(1024)S(1)} %add_rsqrt_fusion.1) | copy-start | bytes 12292
  235.8 10.9 %copy-start.58 = (f32[768]{0:T(1024)S(1)}, f32[768]{0:T(1024)}, u32[]{:S(2)}) copy-start(f32[768]{0:T(1024)} %get-tuple-element.380) | copy-start | bytes 9220
  235.8 10.9 %copy-start.62 = (f32[768]{0:T(1024)S(1)}, f32[768]{0:T(1024)}, u32[]{:S(2)}) copy-start(f32[768]{0:T(1024)} %get-tuple-element.381) | copy-start | bytes 9220
  235.8 10.9 %copy-start.71 = (f32[3072]{0:T(1024)S(1)}, f32[3072]{0:T(1024)}, u32[]{:S(2)}) copy-start(f32[3072]{0:T(1024)} %slice.86) | copy-start | bytes 36868
  246.6 37.0 %copy-start.27 = (bf16[3072,768]{1,0:T(8,128)(2,1)S(1)}, bf16[3072,768]{1,0:T(8,128)(2,1)}, u32[]{:S(2)}) copy-start(bf16[3072,768]{1,0:T(8,128)(2,1)} %reshape.397) | copy-start | bytes 14155780
  246.6 37.0 %copy-start.74 = (f32[768]{0:T(1024)S(1)}, f32[768]{0:T(1024)}, u32[]{:S(2)}) copy-start(f32[768]{0:T(1024)} %get-tuple-element.379) | copy-start | bytes 9220
  292.3 16.4 %slice-start = ((s8[4718592]{0:T(1024)(128)(4,1)}), s8[4194304]{0:T(1024)(128)(4,1)S(1)}, s32[]{:S(2)}) async-start(s8[4718592]{0:T(1024)(128)(4,1)} %bitcast.331), calls=%async_computation.10 | async-start | bytes 8388608
  295.2 13.4 %copy-start.30 = (f32[1024,768]{1,0:T(8,128)}, f32[1024,768]{1,0:T(8,128)S(1)}, u32[]{:S(2)}) copy-start(f32[1024,768]{1,0:T(8,128)S(1)} %get-tuple-element.361) | copy-start | bytes 9437188
  295.2 13.4 %slice-start.1 = ((s8[4718592]{0:T(1024)(128)(4,1)}), s8[524288]{0:T(1024)(128)(4,1)S(1)}, s32[]{:S(2)}) async-start(s8[4718592]{0:T(1024)(128)(4,1)} %bitcast.331), calls=%async_computation.11 | async-start | bytes 1048576
  308.7 6.5 copy-start.20
  338.1 7.2 copy-start.22
  363.9 7.2 copy-start.22
  430.0 347.6 %reduce-scatter.5.cloned.1.call-start = ((), (), s32[]{:S(2)}) async-start(), calls=%async_computation.9 | async-start | bytes 19464192 | tf_op jit(solution)/shard_map/reduce_scatter | solution.py:308
  473.0 13.2 %copy-start.31 = (f32[1024,768]{1,0:T(8,128)S(1)}, f32[1024,768]{1,0:T(8,128)}, u32[]{:S(2)}) copy-start(f32[1024,768]{1,0:T(8,128)} %copy-done.30) | copy-start | bytes 9437188
  569.6 45.7 %all-to-all-start.1 = ((bf16[2,512,768]{2,1,0:T(8,128)(2,1)}), bf16[2,512,768]{2,1,0:T(8,128)(2,1)S(1)}, u32[]{:S(2)}, u32[]{:S(2)}) async-start(bf16[2,512,768]{2,1,0:T(8,128)(2,1)} %bitcast.29), calls=%async_computation.1 | async-start | bytes 3145728 | tf_op jit(solution)/shard_map/all_to_all | solution.py:312
  777.6 45.0 %copy-start.34 = (f32[16,9216]{1,0:T(8,128)S(1)}, f32[16,9216]{1,0:T(8,128)}, u32[]{:S(2)}) copy-start(f32[16,9216]{1,0:T(8,128)} %reduce-scatter.5.cloned.1.call-done) | copy-start | bytes 1769476
  (77 other events, 232.9 us)
Sparse Core Ops, SparseCore 0:
  11.5 66.9 all-gather.2
  82.0 81.3 all-gather.4
  430.1 135.7 reduce-scatter.2
  573.3 204.2 reduce-scatter.4
where the time goes:
time: 855 us; the launch traced here: 845 us
  local copies, waits for them, and re-layouts  276 us (32%)
  matrix products  186 us (22%)
  waiting for transfers between devices  157 us (18%)
  blocking collectives  130 us (15%)
  other arithmetic  63.9 us (7%)
  between operations  19.8 us (2%)
  starting transfers between devices  11.2 us (1%)
    reduce_scatter x1, waiting for transfers between devices, per_device(): lax.psum_scatter(ffn_grad, ('depth', 'dp'), scatter_dimension=0, tiled=True)  156 us
    unnamed x3, blocking collectives  86.1 us
    reshape x4, local copies, waits for them, and re-layouts, to_flat_blocks(): shaped = matrix.reshape(height // BLOCK, BLOCK, breadth // BLOCK, BLOCK)  55.7 us
    dot_general x6, matrix products, product(): return jnp.dot(left, right, preferred_element_type=jnp.float32)  55.2 us
    reshape x6, local copies, waits for them, and re-layouts, to_flat_blocks(): return shaped.transpose(0, 2, 1, 3).reshape(-1, BLOCK * BLOCK)  43.6 us
    psum x1, blocking collectives, per_device(): total = lax.psum(square, ('depth', 'dp'))  39 us
    dot_general x6, matrix products, contract_rows(): lax.dot_general(left, right, (((0,), (0,)), ((), ())), preferred_element_...  35.4 us
    reshape x6, local copies, waits for them, and re-layouts, to_matrix(): return shaped.transpose(0, 2, 1, 3).reshape(height, breadth)  35 us
  transfers between devices with their start and end apart: 7, of which 2 were waited for; matrix products, arithmetic and copies ran while one was open for 30% of the time, Pallas kernels for 0%

commit v1 on v0

--- a/solution.py
+++ b/solution.py
@@ -1,8 +1,11 @@
+import functools
 import math
 
 import jax
 import jax.numpy as jnp
 from jax import lax
+from jax.experimental import pallas as pl
+from jax.experimental.pallas import tpu as pltpu
 from jax.sharding import PartitionSpec as P
 
 HEADS = 12
@@ -140,7 +143,7 @@
     return (first_new, second_new, updated)
 
 
-def per_device(
+def per_device_general(
     inputs,
     output_gradient,
     keep,
@@ -368,9 +371,462 @@
     )
 
 
+MESH = pl.DeviceIdType.MESH
+BF = jnp.bfloat16
+F32 = jnp.float32
+
+
+def place():
+    d = lax.axis_index("depth")
+    i = lax.axis_index("dp")
+    x = i % 2
+    y = (i // 2) % 2
+    z = i // 4
+    c = i % 4
+    nx = i + 1 - 2 * x
+    ny = i + 2 - 4 * y
+    na = ny + d * (nx - ny)
+    nb = nx + d * (ny - nx)
+    return dict(d=d, i=i, z=z, c=c, na=na, nb=nb, ca=na % 4, cb=nb % 4, cd=3 - c)
+
+
+def greet(p):
+    barrier = pltpu.get_barrier_semaphore()
+    peers = [(p["d"], p["na"]), (p["d"], p["nb"]), (1 - p["d"], p["i"])]
+    peers += [(p["d"], ((p["z"] + k) % 4) * 4 + p["c"]) for k in (1, 2, 3)]
+    for peer in peers:
+        pl.semaphore_signal(barrier, inc=1, device_id=peer, device_id_type=MESH)
+    pl.semaphore_wait(barrier, len(peers))
+
+
+def remote(src, dst, send, recv, k, dev):
+    return pltpu.make_async_remote_copy(src_ref=src, dst_ref=dst, send_sem=send.at[k], recv_sem=recv.at[k],
+                                        device_id=dev, device_id_type=MESH)
+
+
+class Spread:
+    def __init__(self, p, own, out, send, recv, local):
+        self.p, self.own, self.out, self.send, self.recv, self.local = p, own, out, send, recv, local
+        self.sent = []
+
+    def go(self, src, dst, k, dev):
+        copy = remote(src, dst, self.send, self.recv, k, dev)
+        copy.start()
+        self.sent.append(copy)
+
+    def start(self):
+        p = self.p
+        here = self.out.at[p["d"], p["z"], p["c"]]
+        self.keep = pltpu.make_async_copy(self.own, here, self.local)
+        self.keep.start()
+        for k in (2, 1, 3):
+            self.go(self.own, here, k - 1, (p["d"], ((p["z"] + k) % 4) * 4 + p["c"]))
+
+    def wait(self, dst, k):
+        remote(dst, dst, self.send, self.recv, k, (self.p["d"], self.p["na"])).wait_recv()
+
+    def column(self, half, col):
+        return self.out.at[half, :, col]
+
+    def second(self):
+        p = self.p
+        self.keep.wait()
+        for k in (1, 2, 3):
+            self.wait(self.out.at[p["d"], (p["z"] + 4 - k) % 4, p["c"]], k - 1)
+        mine = self.column(p["d"], p["c"])
+        self.go(mine, mine, 3, (p["d"], p["na"]))
+        self.go(mine, mine, 4, (p["d"], p["nb"]))
+        self.go(mine, mine, 6, (1 - p["d"], p["i"]))
+
+    def third(self):
+        p = self.p
+        got = self.column(p["d"], p["ca"])
+        self.wait(got, 3)
+        self.go(got, got, 5, (p["d"], p["nb"]))
+        self.go(got, got, 8 - p["d"], (1 - p["d"], p["i"]))
+
+    def fourth(self):
+        p = self.p
+        got = self.column(p["d"], p["cb"])
+        self.wait(got, 4)
+        self.go(got, got, 7 + p["d"], (1 - p["d"], p["i"]))
+
+    def fifth(self):
+        p = self.p
+        got = self.column(p["d"], p["cd"])
+        self.wait(got, 5)
+        self.go(got, got, 9, (1 - p["d"], p["i"]))
+
+    def sixth(self):
+        p = self.p
+        for k, col in ((6, p["c"]), (8 - p["d"], p["ca"]), (7 + p["d"], p["cb"]), (9, p["cd"])):
+            self.wait(self.column(1 - p["d"], col), k)
+
+    def drain(self):
+        for copy in self.sent:
+            copy.wait_send()
+
+
+def gather_kernel(a, v, f, ga, gv, gf, *sems):
+    p = place()
+    greet(p)
+    parts = [Spread(p, own, out, sems[3 * n], sems[3 * n + 1], sems[3 * n + 2])
+             for n, (own, out) in enumerate(((a, ga), (v, gv), (f, gf)))]
+    for s in parts:
+        s.start()
+    for s in parts[:2]:
+        s.second()
+    for s in parts[:2]:
+        s.third()
+    for s in parts[:2]:
+        s.fourth()
+    parts[2].second()
+    for s in parts[:2]:
+        s.fifth()
+    parts[2].third()
+    parts[2].fourth()
+    parts[2].fifth()
+    for s in parts:
+        s.sixth()
+    for s in parts:
+        s.drain()
+
+
+def gather(a, v, f):
+    sem = [pltpu.SemaphoreType.DMA((10,)), pltpu.SemaphoreType.DMA((10,)), pltpu.SemaphoreType.DMA]
+    return pl.pallas_call(
+        gather_kernel,
+        out_shape=[jax.ShapeDtypeStruct((2, 4, 4) + t.shape, t.dtype) for t in (a, v, f)],
+        in_specs=[pl.BlockSpec(memory_space=pltpu.VMEM)] * 3,
+        out_specs=[pl.BlockSpec(memory_space=pl.ANY)] * 3,
+        scratch_shapes=sem * 3,
+        compiler_params=pltpu.CompilerParams(collective_id=0, has_side_effects=True),
+        name="weight_gather",
+    )(a, v, f)
+
+
+class Fold:
+    def __init__(self, p, mine, pair, diag, flat, late, line, send, recv):
+        self.p, self.mine, self.pair, self.diag, self.flat, self.late, self.line = p, mine, pair, diag, flat, late, line
+        self.send, self.recv, self.sent = send, recv, []
+
+    def go(self, src, dst, k, dev):
+        copy = remote(src, dst, self.send, self.recv, k, dev)
+        copy.start()
+        self.sent.append(copy)
+
+    def wait(self, dst, k):
+        remote(dst, dst, self.send, self.recv, k, (self.p["d"], self.p["na"])).wait_recv()
+
+    def add(self, dst, *others):
+        total = dst[...].astype(F32)
+        for o in others:
+            total += o[...].astype(F32)
+        dst[...] = total.astype(dst.dtype)
+
+    def start(self):
+        p = self.p
+        self.go(self.mine.at[1 - p["d"]], self.pair, 0, (1 - p["d"], p["i"]))
+
+    def second(self):
+        p = self.p
+        self.wait(self.pair, 0)
+        for col, dst, k in ((p["cd"], self.diag, 1), (p["cb"], self.flat, 2)):
+            self.add(self.pair.at[:, col], self.mine.at[p["d"], :, col])
+            self.go(self.pair.at[:, col], dst, k, (p["d"], p["nb"]))
+        for col in (p["ca"], p["c"]):
+            self.add(self.pair.at[:, col], self.mine.at[p["d"], :, col])
+
+    def third(self):
+        p = self.p
+        self.wait(self.diag, 1)
+        src = self.pair.at[:, p["ca"]]
+        self.add(src, self.diag)
+        self.go(src, self.late, 3, (p["d"], p["na"]))
+
+    def fourth(self):
+        p = self.p
+        self.wait(self.flat, 2)
+        self.wait(self.late, 3)
+        for k in (2, 1, 3, 0):
+            dst = (p["z"] + k) % 4
+            self.add(self.pair.at[dst, p["c"]], self.flat.at[dst], self.late.at[dst])
+            if k:
+                self.go(self.pair.at[dst, p["c"]], self.line.at[k - 1], 3 + k, (p["d"], dst * 4 + p["c"]))
+
+    def fifth(self, out):
+        p = self.p
+        total = self.pair[p["z"], p["c"]].astype(F32)
+        for k in (1, 2, 3):
+            self.wait(self.line.at[k - 1], 3 + k)
+            total += self.line[k - 1].astype(F32)
+        out[...] = total
+
+    def drain(self):
+        for copy in self.sent:
+            copy.wait_send()
+
+
+def fold_scratch(shape, dtype):
+    return [pltpu.VMEM((4, 4) + shape, dtype), pltpu.VMEM((4,) + shape, dtype), pltpu.VMEM((4,) + shape, dtype),
+            pltpu.VMEM((4,) + shape, dtype), pltpu.VMEM((3,) + shape, dtype),
+            pltpu.SemaphoreType.DMA((7,)), pltpu.SemaphoreType.DMA((7,))]
+
+
+def greet_all(p):
+    barrier = pltpu.get_barrier_semaphore()
+    me = p["d"] * 16 + p["i"]
+    for k in range(1, 32):
+        t = (me + k) % 32
+        pl.semaphore_signal(barrier, inc=1, device_id=(t // 16, t % 16), device_id_type=MESH)
+    pl.semaphore_wait(barrier, 31)
+
+
+def norm_sum(p, square, slots, send, recv):
+    me = p["d"] * 16 + p["i"]
+    slots[0] = jnp.full((8, 128), square, F32)
+    copies = []
+    for k in range(1, 32):
+        t = (me + k) % 32
+        copy = remote(slots.at[0], slots.at[k], send, recv, k, (t // 16, t % 16))
+        copy.start()
+        copies.append(copy)
+    for copy in copies:
+        copy.wait_recv()
+    total = jnp.sum(slots[...], axis=0)[0:1, 0:1]
+    for copy in copies:
+        copy.wait_send()
+    return total
+
+
+def scatter_kernel(f, a, v, bf, ba, sv, norm, sf, sa, slots, nsend, nrecv, *scratch):
+    p = place()
+    greet_all(p)
+    parts = [Fold(p, mine, *scratch[7 * n:7 * n + 7]) for n, mine in enumerate((f, a, v))]
+    for step in ("start", "second", "third", "fourth"):
+        for s in parts:
+            getattr(s, step)()
+    for s, out in zip(parts, (sf, sa, sv)):
+        s.fifth(out)
+    square = jnp.sum(sa[...] * sa[...]) + jnp.sum(sf[...] * sf[...]) + jnp.sum(sv[...] * sv[...])
+    total = norm_sum(p, square, slots, nsend, nrecv)
+    norm[...] = jnp.sqrt(total)
+    for b in range(8):
+        ba[b] = sa[:, b * BLOCK:(b + 1) * BLOCK]
+        for j in range(2):
+            bf[8 * j + b] = sf[j, :, b * BLOCK:(b + 1) * BLOCK]
+    for s in parts:
+        s.drain()
+
+
+def scatter(f, a, v):
+    outs = [jax.ShapeDtypeStruct(s, F32) for s in ((16, BLOCK, BLOCK), (8, BLOCK, BLOCK), v.shape[3:], (1, 1))]
+    return pl.pallas_call(
+        scatter_kernel,
+        out_shape=outs,
+        in_specs=[pl.BlockSpec(memory_space=pltpu.VMEM)] * 3,
+        out_specs=[pl.BlockSpec(memory_space=pltpu.VMEM)] * 4,
+        scratch_shapes=[pltpu.VMEM(f.shape[3:], F32), pltpu.VMEM(a.shape[3:], F32), pltpu.VMEM((32, 8, 128), F32),
+                        pltpu.SemaphoreType.DMA((32,)), pltpu.SemaphoreType.DMA((32,))]
+        + sum((fold_scratch(t.shape[3:], t.dtype) for t in (f, a, v)), []),
+        compiler_params=pltpu.CompilerParams(collective_id=1, has_side_effects=True, vmem_limit_bytes=60 << 20),
+        name="grad_scatter",
+    )(f, a, v)
+
+
+TOP = lax.Precision.HIGHEST
+
+
+def shampoo_block(grad, w, st, ro, mo, st_new, mo_new, w_new, b, factor):
+    clipped = grad * factor
+    moment = momentum_decay * mo[b] + clipped
+    left = lax.dot_general(clipped, clipped, (((1,), (1,)), ((), ())), precision=TOP, preferred_element_type=F32)
+    right = lax.dot_general(clipped, clipped, (((0,), (0,)), ((), ())), precision=TOP, preferred_element_type=F32)
+    st_new[b, 0] = stat_decay * st[b, 0] + (1.0 - stat_decay) * left
+    st_new[b, 1] = stat_decay * st[b, 1] + (1.0 - stat_decay) * right
+    mo_new[b] = moment
+    turned = jnp.dot(ro[b, 0], moment, precision=TOP, preferred_element_type=F32)
+    turned = jnp.dot(turned, ro[b, 1], precision=TOP, preferred_element_type=F32)
+    w_new[b] = w[b] - matrix_rate * (turned + matrix_decay * w[b])
+
+
+def optimizer_kernel(norm, ga, gf, sv, aw, ast, ar, am, fw, fst, fr, fm, vw, v1, v2,
+                     ast_n, am_n, aw_n, fst_n, fm_n, fw_n, v1_n, v2_n, vw_n):
+    factor = clip_bound / jnp.maximum(norm[...], clip_bound)
+    shampoo_block(ga[0], aw, ast, ar, am, ast_n, am_n, aw_n, 0, factor)
+    shampoo_block(gf[0], fw, fst, fr, fm, fst_n, fm_n, fw_n, 0, factor)
+    shampoo_block(gf[1], fw, fst, fr, fm, fst_n, fm_n, fw_n, 1, factor)
+
+    @pl.when(pl.program_id(0) == 0)
+    def _():
+        size = vw.shape[0]
+        clipped = (sv[0:1, 0:size] * factor)[0]
+        first_new = first_decay * v1[...] + (1.0 - first_decay) * clipped
+        second_new = second_decay * v2[...] + (1.0 - second_decay) * clipped * clipped
+        first_hat = first_new / (1.0 - first_decay**STEP)
+        second_hat = second_new / (1.0 - second_decay**STEP)
+        v1_n[...] = first_new
+        v2_n[...] = second_new
+        vw_n[...] = vw[...] - vector_rate * first_hat / (jnp.sqrt(second_hat) + adam_floor)
+
+
+def optimizer(norm, ga, gf, sv, aw, ast, ar, am, fw, fst, fr, fm, vw, v1, v2):
+    def steps(t, n):
+        shape = (n,) + t.shape[1:]
+        return pl.BlockSpec(shape, lambda g: (g,) + (0,) * (len(shape) - 1))
+
+    def whole(t):
+        return pl.BlockSpec(t.shape, lambda g: (0,) * t.ndim)
+
+    like = lambda t: jax.ShapeDtypeStruct(t.shape, F32)
+    args = (norm, ga, gf, sv, aw, ast, ar, am, fw, fst, fr, fm, vw, v1, v2)
+    specs = [whole(norm), steps(ga, 1), steps(gf, 2), whole(sv)]
+    specs += [steps(t, 1) for t in (aw, ast, ar, am)] + [steps(t, 2) for t in (fw, fst, fr, fm)]
+    specs += [whole(t) for t in (vw, v1, v2)]
+    outs = (ast, am, aw, fst, fm, fw, v1, v2, vw)
+    return pl.pallas_call(
+        optimizer_kernel,
+        out_shape=[like(t) for t in outs],
+        grid=(8,),
+        in_specs=specs,
+        out_specs=[steps(t, 1) for t in outs[:3]] + [steps(t, 2) for t in outs[3:6]] + [whole(t) for t in outs[6:]],
+        name="optimizer",
+    )(*args)
+
+
+def per_device(
+    inputs,
+    output_gradient,
+    keep,
+    lengths,
+    routes,
+    attn_weights,
+    attn_stats,
+    attn_roots,
+    attn_momentum,
+    ffn_weights,
+    ffn_stats,
+    ffn_roots,
+    ffn_momentum,
+    vec_weights,
+    vec_first,
+    vec_second,
+):
+    slots, seq_len, width = inputs.shape
+    tokens = slots * seq_len
+    head_size = width // HEADS
+    per_row = width // BLOCK
+    share = vec_weights.shape[0]
+    strip = attn_weights.astype(BF).transpose(1, 0, 2).reshape(BLOCK, width)
+    pair = ffn_weights.astype(BF).reshape(2, per_row, BLOCK, BLOCK).transpose(0, 2, 1, 3).reshape(2, BLOCK, width)
+    vec = jnp.pad(vec_weights.astype(BF).astype(F32)[None], ((0, 7), (0, 96)))
+    ga, gv, gf = gather(strip, vec, pair)
+    attn = ga.reshape(4, width, width)
+    query_w, key_w, value_w, output_w = attn[0], attn[1], attn[2], attn[3]
+    up = gf[0].reshape(4, 2, 2, 2, BLOCK, width).transpose(0, 1, 4, 2, 3, 5).reshape(width, FF)
+    down = gf[1].reshape(FF, width)
+    vectors = gv[..., 0, :share].reshape(-1)
+    q_bias, v_bias, out_bias = (vectors[n * width:(n + 1) * width] for n in range(3))
+    hidden_bias = vectors[3 * width:3 * width + FF]
+    ffn_bias, gain_one, shift_one, gain_two, shift_two = (
+        vectors[n * width + FF:(n + 1) * width + FF] for n in range(3, 8)
+    )
+    served = serve_flags(keep[None, :], routes[None, :])[0]
+    flat = inputs.reshape(tokens, width)
+    four = (slots, seq_len, HEADS, head_size)
+    query = (product(flat, query_w) + q_bias).astype(BF).reshape(four)
+    keys = product(flat, key_w).astype(BF).reshape(four)
+    values = (product(flat, value_w) + v_bias).astype(BF).reshape(four)
+    context, log_total = lax.map(attend_forward, (query, keys, values, lengths))
+    context_low = context.reshape(tokens, width).astype(BF)
+    attended = product(context_low, output_w) + out_bias
+    normed_one, factor_one = norm_parts(flat.astype(F32) + attended)
+    hidden_in = normed_one * gain_one + shift_one
+    hidden_low = hidden_in.astype(BF)
+    before = product(hidden_low, up) + hidden_bias
+    active_low = jax.nn.gelu(before, approximate=False).astype(BF)
+    branch = product(active_low, down) + ffn_bias
+    normed_two, factor_two = norm_parts(hidden_in + branch)
+    result = normed_two * gain_two + shift_two
+    flag = jnp.repeat(served, seq_len)[:, None] > 0
+    grad_flat = output_gradient.reshape(tokens, width)
+    grad_rows = jnp.where(flag, grad_flat.astype(F32), 0.0)
+    grad_gain_two = jnp.sum(grad_rows * normed_two, axis=0)
+    grad_shift_two = jnp.sum(grad_rows, axis=0)
+    grad_resid_two = norm_back(grad_rows * gain_two, normed_two, factor_two)
+    grad_branch = grad_resid_two.astype(BF)
+    grad_ffn_bias = jnp.sum(grad_branch.astype(F32), axis=0)
+    grad_down = contract_rows(active_low, grad_branch)
+    grad_active = times_transpose(grad_branch, down)
+    grad_before = (grad_active * gelu_slope(before)).astype(BF)
+    grad_hidden_bias = jnp.sum(grad_before.astype(F32), axis=0)
+    grad_up = contract_rows(hidden_low, grad_before)
+    grad_hidden = times_transpose(grad_before, up) + grad_resid_two
+    grad_gain_one = jnp.sum(grad_hidden * normed_one, axis=0)
+    grad_shift_one = jnp.sum(grad_hidden, axis=0)
+    grad_resid_one = norm_back(grad_hidden * gain_one, normed_one, factor_one)
+    grad_attended = grad_resid_one.astype(BF)
+    grad_out_bias = jnp.sum(grad_attended.astype(F32), axis=0)
+    grad_output_w = contract_rows(context_low, grad_attended)
+    grad_context = times_transpose(grad_attended, output_w).astype(BF).reshape(four)
+    grad_query, grad_keys, grad_values = lax.map(
+        attend_backward, (query, keys, values, grad_context, log_total, lengths)
+    )
+    grad_query = grad_query.reshape(tokens, width).astype(BF)
+    grad_keys = grad_keys.reshape(tokens, width).astype(BF)
+    grad_values = grad_values.reshape(tokens, width).astype(BF)
+    grad_q_bias = jnp.sum(grad_query.astype(F32), axis=0)
+    grad_v_bias = jnp.sum(grad_values.astype(F32), axis=0)
+    in_rows = (
+        grad_resid_one
+        + times_transpose(grad_query, query_w)
+        + times_transpose(grad_keys, key_w)
+        + times_transpose(grad_values, value_w)
+    )
+    out = jnp.where(flag, result.astype(BF), flat).reshape(inputs.shape)
+    in_grad = jnp.where(flag, in_rows.astype(BF), grad_flat).reshape(inputs.shape)
+    ha = jnp.stack(
+        [
+            contract_rows(flat, grad_query).astype(BF),
+            contract_rows(flat, grad_keys).astype(BF),
+            contract_rows(flat, grad_values).astype(BF),
+            grad_output_w.astype(BF),
+        ]
+    ).reshape(2, 4, 4, BLOCK, width)
+    hf = jnp.stack(
+        [
+            grad_up.astype(BF).reshape(4, 2, BLOCK, 2, 2, width).transpose(0, 1, 3, 4, 2, 5).reshape(4, 4, 2, BLOCK, width),
+            grad_down.astype(BF).reshape(4, 4, 2, BLOCK, width),
+        ]
+    )
+    vec_grad = jnp.concatenate(
+        [
+            grad_q_bias,
+            grad_v_bias,
+            grad_out_bias,
+            grad_hidden_bias,
+            grad_ffn_bias,
+            grad_gain_one,
+            grad_shift_one,
+            grad_gain_two,
+            grad_shift_two,
+        ]
+    )
+    hv = jnp.pad(vec_grad.reshape(2, 4, 4, 1, share), ((0, 0),) * 3 + ((0, 7), (0, 96)))
+    bf, ba, sv, norm = scatter(hf, ha, hv)
+    rest = optimizer(
+        norm, ba, bf, sv,
+        attn_weights, attn_stats, attn_roots, attn_momentum,
+        ffn_weights, ffn_stats, ffn_roots, ffn_momentum,
+        vec_weights, vec_first, vec_second,
+    )
+    return (out, in_grad, norm.reshape(()), *rest)
+
+
 def solution(mesh):
+    small = mesh.shape["depth"] == 2 and mesh.shape["dp"] == 16
     return jax.shard_map(
-        per_device,
+        per_device if small else per_device_general,
         mesh=mesh,
         in_specs=(
             P(("depth", "dp"), None, None),

time: 855 us -> 555 us (0.65)
  Pallas kernels: 0 us -> 233 us
  local copies, waits for them, and re-layouts: 276 us -> 93.8 us
  waiting for transfers between devices: 157 us -> 0 us
  blocking collectives: 130 us -> 0 us
  matrix products: 186 us -> 164 us
  between operations: 19.8 us -> 3.47 us
  other arithmetic: 63.9 us -> 50.7 us
  starting transfers between devices: 11.2 us -> 0 us
    pallas_call x0 -> x3, Pallas kernels: none -> 233 us  [the longest x1 131 us: scatter(): pl.pallas_call(scatter_kernel, out_shape=outs, in_specs=[pl.BlockSpec(mem...]
    reduce_scatter x2 -> x0, waiting for transfers between devices: 156 us -> none  [the longest x1 156 us: per_device(): lax.psum_scatter(ffn_grad, ('depth', 'dp'), scatter_dimension=0, tiled=True)]
    reshape x26 -> x11, local copies, waits for them, and re-layouts: 174 us -> 38.3 us  [the longest x2 17.3 us: per_device(): grad_up.astype(BF).reshape(4, 2, BLOCK, 2, 2, width)]
    unnamed x3 -> x0, blocking collectives: 86.1 us -> none
    psum x1 -> x0, blocking collectives: 39 us -> none  [per_device(): total = lax.psum(square, ('depth', 'dp'))]
    transpose x6 -> x1, local copies, waits for them, and re-layouts: 23.5 us -> 0.08 us  [per_device(): strip = attn_weights.astype(BF).transpose(1, 0, 2).reshape(BLOCK, width)]
    concatenate x2 -> x0, other arithmetic: 21.7 us -> none  [the longest x1 14.4 us: per_device(): jnp.concatenate([to_flat_blocks(grad_hidden_w), to_flat_blocks(gradient_r...]
    dot_general x12 -> x0, matrix products: 21.3 us -> none  [the longest x1 4.87 us: per_device(): jnp.einsum('rx,rmp->xmp', selection, returned_rows, preferred_element_typ...]
  transfers between devices with their start and end apart: 7 -> 0, of which waited for: 2 -> 0; matrix products, arithmetic and copies ran while one was open for 30% -> 0% of each run, Pallas kernels for 0% -> 0%
where the time goes in v1:
time: 555 us; the launch traced here: 547 us
  Pallas kernels  233 us (42%)
  matrix products  164 us (30%)
  local copies, waits for them, and re-layouts  93.8 us (17%)
  other arithmetic  50.7 us (9%)
    pallas_call x1, Pallas kernels, scatter(): pl.pallas_call(scatter_kernel, out_shape=outs, in_specs=[pl.BlockSpec(mem...  131 us
    pallas_call x1, Pallas kernels, gather(): pl.pallas_call(gather_kernel, out_shape=[jax.ShapeDtypeStruct((2, 4, 4) +...  87.9 us
    dot_general x6, matrix products, product(): return jnp.dot(left, right, preferred_element_type=jnp.float32)  59.9 us
    dot_general x6, matrix products, times_transpose(): lax.dot_general(left, right, (((1,), (1,)), ((), ())), preferred_element_...  33 us
    dot_general x6, matrix products, contract_rows(): lax.dot_general(left, right, (((0,), (0,)), ((), ())), preferred_element_...  26.3 us
    reshape x2, local copies, waits for them, and re-layouts, per_device(): grad_up.astype(BF).reshape(4, 2, BLOCK, 2, 2, width)  17.3 us
    convert_element_type x2, other arithmetic, attend_backward(): grad_scores = (probs * (grad_probs - along)).astype(jnp.bfloat16)  14.5 us
    dot_general x2, matrix products, attend_backward(): jnp.einsum('qhe,khe->hqk', grad_ctx, values, preferred_element_type=jnp.f...  14.5 us

profile of v1, /device:TPU:0, one launch (start us, length us, event | category | flops | bytes accessed | tf_op | source)
XLA Modules:
  0.0 546.8 jit_solution(4552425555414872870)
XLA Ops:
  8.7 87.9 %weight_gather.1 = (bf16[2,4,4,96,768]{4,3,2,1,0:T(8,128)(2,1)}, f32[2,4,4,8,384]{4,3,2,1,0:T(8,128)}, bf16[2,4,4,2,96,768]{5,4,3,2,1,0:T(8,128)(2,1)}) custom-call(bf16[96,768]{1,0:T(8,128)(2,1)} %reshape.302.a, f32[8,384]{1,0:T(8,128)} %pad_convert_fusion.v, bf16[2,96,768]{2,1,0:T(8,128)(2,1)} %reshape.304.f), custom_call_target="tpu_custom_call" | custom-call | tf_op jit(solution)/shard_map/weight_gather/pallas_call | solution.py:497
  106.2 3.9 fusion.64
  122.9 24.1 %while.26 = (s32[]{:T(128)}, bf16[2,512,12,64]{1,3,2,0:T(8,128)(2,1)}, f32[2,12,512]{2,1,0:T(8,128)}, bf16[2,512,12,64]{1,3,2,0:T(8,128)(2,1)}, s32[2]{0:T(128)S...) while((s32[]{:T(128)}, ...), condition=%wide.region_4.5_spmd, body=%wide.region_1.4_spmd.sunk | while | flops 843049472 | bytes 48197772 | solution.py:740
  124.6 3.1 fusion.123
  130.3 4.2 bitcast_dynamic-update-slice_fusion.10
  136.3 3.1 fusion.123
  142.1 4.2 bitcast_dynamic-update-slice_fusion.10
  147.0 4.2 copy.71
  151.7 3.5 fusion.84
  155.7 8.4 %fusion.82 = (bf16[1,4,4,2,96,768]{5,4,3,2,1,0:T(8,128)(2,1)}, bf16[1,4,4,2,96,768]{5,4,3,2,1,0:T(8,128)(2,1)}) fusion(bf16[2,4,4,2,96,768]{5,4,3,2,1,0:T(8,128)(2,1)} %get-tuple-element.123), kind=kLoop, calls=%fused_computation.168 | loop fusion | bytes 18874368 | tf_op jit(solution)/shard_map/slice | solution.py:727
  164.1 9.4 %copy.93 = bf16[4,2,2,2,96,768]{5,3,2,4,1,0:T(2,128)(2,1)} copy(bf16[4,2,2,2,96,768]{5,4,3,2,1,0:T(8,128)(2,1)} %bitcast.222) | data formatting | bytes 9437184 | tf_op jit(solution)/shard_map/reshape;squeeze | solution.py:726
  173.5 11.3 %reshape.309 = bf16[768,3072]{1,0:T(8,128)(2,1)} reshape(bf16[4,2,96,2,2,768]{5,4,3,2,1,0:T(2,128)(2,1)} %bitcast.221) | data formatting | bytes 9437184 | tf_op jit(solution)/shard_map/reshape | solution.py:726
  184.8 37.0 %fusion.45 = (bf16[1024,3072]{1,0:T(8,128)(2,1)S(1)}, f32[1024,3072]{1,0:T(8,128)}) fusion(f32[3072]{0:T(1024)S(1)} %copy-done.47, bf16[768,3072]{1,0:T(8,128)(2,1)} %reshape.309, f32[1024,768]{1,0:T(8,128)S(1)} %get-tuple-element.253, f32[768]{0:T(1024)S(1)} %copy-done.48, f32[768]{0:T(1024)S(1)} %copy-done.41, f32[1024]{0:T(1024)S(1)} %add_rsqrt_fusion.1, ...), kind=kOutput, calls=%fused_computation.58 | convolution fusion | flops 5043388416 | bytes 26765312 | tf_op jit(solution)/shard_map/dot_general | solution.py:69
  221.9 10.0 %fusion.85 = (f32[1024]{0:T(1024)S(1)}, f32[1024,768]{1,0:T(8,128)S(1)}) fusion(f32[768]{0:T(1024)S(1)} %copy-done.49, bf16[1024,3072]{1,0:T(8,128)(2,1)S(1)} %get-tuple-element.254, bf16[3072,768]{1,0:T(8,128)(2,1)} %bitcast.232, f32[768]{0:T(1024)S(1)} %copy-done.48, f32[768]{0:T(1024)S(1)} %copy-done.41, f32[1024]{0:T(1024)S(1)} %add_rsqrt_fusion.1, ...), kind=kOutput, calls=%fused_computation.171 | convolution fusion | flops 4837342208 | bytes 17323008 | tf_op jit(solution)/shard_map/dot_general | solution.py:69
  239.8 12.3 %convert_reduce_fusion = (f32[3072]{0:T(1024)}, bf16[1024,3072]{1,0:T(8,128)(2,1)S(1)}) fusion(f32[1024,3072]{1,0:T(8,128)} %get-tuple-element.255, f32[3072]{0:T(1024)S(1)} %copy-done.47, bf16[3072,768]{1,0:T(8,128)(2,1)S(1)} %bitcast.235, f32[1024,768]{1,0:T(8,128)S(1)} %get-tuple-element.235), kind=kOutput, calls=%fused_computation.65 | convolution fusion | flops 4873516032 | bytes 26763264 | tf_op jit(solution)/shard_map/dot_general | solution.py:79
  252.1 10.0 %convolution_convert_fusion = bf16[3072,768]{1,0:T(8,128)(2,1)} fusion(bf16[1024,3072]{1,0:T(8,128)(2,1)} %copy-done.54, f32[1024,768]{1,0:T(8,128)S(1)} %get-tuple-element.235), kind=kOutput, calls=%fused_computation.82 | convolution fusion | flops 4834983936 | bytes 14155776 | tf_op jit(solution)/shard_map/dot_general | solution.py:73
  262.2 6.5 %multiply_reduce_fusion.2 = (f32[768]{0:T(1024)}, f32[1024]{0:T(1024)S(1)}, f32[1024]{0:T(1024)S(1)}, f32[768]{0:T(1024)}, f32[1024,768]{1,0:T(8,128)S(1)}) fusion(f32[1024,768]{1,0:T(8,128)S(1)} %get-tuple-element.253, f32[1024]{0:T(1024)S(1)} %add_rsqrt_fusion.1, f32[1024]{0:T(1024)S(1)} %broadcast_multiply_fusion.4, f32[768]{0:T(1024)S(1)} %copy-done.41, ...), kind=kOutput, calls=%fused_computation.87 | convolution fusion | flops 4839698432 | bytes 20472832 | tf_op jit(solution)/shard_map/dot_general | solution.py:79
  270.4 7.9 %convolution_convert_fusion.1 = bf16[768,3072]{1,0:T(8,128)(2,1)} fusion(bf16[1024,3072]{1,0:T(8,128)(2,1)S(1)} %get-tuple-element.260, f32[1024,768]{1,0:T(8,128)S(1)} %get-tuple-element.253, f32[768]{0:T(1024)S(1)} %copy-done.48, f32[768]{0:T(1024)S(1)} %copy-done.41, f32[1024]{0:T(1024)S(1)} %add_rsqrt_fusion.1, f32[1024]{0:T(1024)S(1)} %broadcast_multiply_fusion.4), kind=kOutput, calls=%fused_computation.83 | convolution fusion | flops 4838129664 | bytes 14170112 | tf_op jit(solution)/shard_map/dot_general | solution.py:73
  280.8 11.8 %reshape.314 = bf16[4,2,96,2,2,768]{5,4,3,2,1,0:T(2,128)(2,1)} reshape(bf16[768,3072]{1,0:T(8,128)(2,1)} %convolution_convert_fusion.1) | data formatting | bytes 9437184 | tf_op jit(solution)/shard_map/reshape | solution.py:798
  292.6 5.5 copy.81
  298.0 8.3 %pad_maximum_fusion.f = bf16[2,4,4,2,96,768]{5,4,3,2,1,0:T(8,128)(2,1)} fusion(bf16[1,4,4,2,96,768]{5,4,3,2,1,0:T(8,128)(2,1)} %bitcast.236, bf16[1,4,4,2,96,768]{5,4,3,2,1,0:T(8,128)(2,1)} %bitcast.223), kind=kLoop, calls=%fused_computation.81 | loop fusion | flops 4718592 | bytes 18874368 | tf_op jit(solution)/shard_map/stack | solution.py:796
  306.4 3.8 convolution_convert_fusion.2
  318.7 50.6 %while.27 = (s32[]{:T(128)}, bf16[2,512,12,64]{1,3,2,0:T(8,128)(2,1)}, bf16[2,512,12,64]{1,3,2,0:T(8,128)(2,1)}, bf16[2,512,12,64]{1,3,2,0:T(8,128)(2,1)}, bf16[...) while((s32[]{:T(128)}, ...), condition=%wide.region_15.16_spmd, body=%wide.region_13.15_spmd.sunk | while | flops 2061232640 | bytes 155123088 | solution.py:772
  321.9 3.1 bitcast_dynamic-update-slice_fusion.14
  325.0 7.2 %multiply_reduce_fusion.10 = (f32[12,512]{1,0:T(8,128)S(1)}, f32[12,512,512]{1,2,0:T(8,128)}) fusion(f32[12,512,512]{1,2,0:T(8,128)S(1)} %fusion.133, f32[12,512]{1,0:T(8,128)S(1)} %dynamic-slice_bitcast_fusion.2, pred[512]{0:T(512)(128)(4,1)S(1)} %iota_compare_fusion.5, bf16[2,512,12,64]{1,3,2,0:T(8,128)(2,1)S(1)} %copy-done.8, s32[]{:T(128)S(6)} %copy.113, ...), kind=kOutput, calls=%fused_computation.21.clone.1 | convolution fusion | flops 418375680 | bytes 26797568 | tf_op jit(solution)/shard_map/while/body/eval_jaxpr/qhe,khe->hqk/dot_general | solution.py:108
  332.2 7.2 %multiply_convert_fusion.2 = bf16[12,512,512]{1,2,0:T(8,128)(2,1)S(1)} fusion(f32[12,512,512]{1,2,0:T(8,128)} %get-tuple-element.373, f32[12,512,512]{1,2,0:T(8,128)S(1)} %fusion.133, f32[12,512]{1,0:T(8,128)S(1)} %get-tuple-element.374, f32[12,512]{1,0:T(8,128)S(1)} %dynamic-slice_bitcast_fusion.2, pred[512]{0:T(512)(128)(4,1)S(1)} %iota_compare_fusion.5), kind=kLoop, calls=%fused_computation.20.clone.1 | loop fusion | flops 18874368 | bytes 31506944 | tf_op jit(solution)/shard_map/while/body/eval_jaxpr/convert_element_type | solution.py:113
  350.1 7.2 %multiply_reduce_fusion.10 = (f32[12,512]{1,0:T(8,128)S(1)}, f32[12,512,512]{1,2,0:T(8,128)}) fusion(f32[12,512,512]{1,2,0:T(8,128)S(1)} %fusion.133, f32[12,512]{1,0:T(8,128)S(1)} %dynamic-slice_bitcast_fusion.2, pred[512]{0:T(512)(128)(4,1)S(1)} %iota_compare_fusion.5, bf16[2,512,12,64]{1,3,2,0:T(8,128)(2,1)S(1)} %copy-done.8, s32[]{:T(128)S(6)} %copy.113, ...), kind=kOutput, calls=%fused_computation.21.clone.1 | convolution fusion | flops 418375680 | bytes 26797568 | tf_op jit(solution)/shard_map/while/body/eval_jaxpr/qhe,khe->hqk/dot_general | solution.py:108
  357.3 7.2 %multiply_convert_fusion.2 = bf16[12,512,512]{1,2,0:T(8,128)(2,1)S(1)} fusion(f32[12,512,512]{1,2,0:T(8,128)} %get-tuple-element.373, f32[12,512,512]{1,2,0:T(8,128)S(1)} %fusion.133, f32[12,512]{1,0:T(8,128)S(1)} %get-tuple-element.374, f32[12,512]{1,0:T(8,128)S(1)} %dynamic-slice_bitcast_fusion.2, pred[512]{0:T(512)(128)(4,1)S(1)} %iota_compare_fusion.5), kind=kLoop, calls=%fused_computation.20.clone.1 | loop fusion | flops 18874368 | bytes 31506944 | tf_op jit(solution)/shard_map/while/body/eval_jaxpr/convert_element_type | solution.py:113
  369.4 3.1 copy.79
  389.1 131.3 %grad_scatter.1 = (f32[16,96,96]{2,1,0:T(8,128)}, f32[8,96,96]{2,1,0:T(8,128)}, f32[8,384]{1,0:T(8,128)}, f32[1,1]{1,0:T(1,128)}) custom-call(bf16[2,4,4,2,96,768]{5,4,3,2,1,0:T(8,128)(2,1)} %pad_maximum_fusion.f, bf16[2,4,4,96,768]{4,3,2,1,0:T(8,128)(2,1)} %bitcast.220, f32[2,4,4,8,384]{4,3,2,1,0:T(8,128)} %pad.12.v), custom_call_target="tpu_custom_call" | custom-call | tf_op jit(solution)/shard_map/grad_scatter/pallas_call | solution.py:624
  526.2 4.6 bitcast_select_fusion
  530.8 14.0 %optimizer.1 = (f32[8,2,96,96]{3,2,1,0:T(8,128)}, f32[8,96,96]{2,1,0:T(8,128)}, f32[8,96,96]{2,1,0:T(8,128)}, f32[16,2,96,96]{3,2,1,0:T(8,128)}, f32[16,96,96]{2...) custom-call(f32[1,1]{1,0:T(1,128)} %get-tuple-element.128.norm, ...), custom_call_target="tpu_custom_call" | custom-call | tf_op jit(solution)/shard_map/optimizer/pallas_call | solution.py:687
  (236 shorter events, 100.6 us)
Async XLA Ops:
  0.6 98.4 %copy-start.4 = (bf16[2,512,768]{2,1,0:T(8,128)(2,1)S(1)}, bf16[2,512,768]{2,1,0:T(8,128)(2,1)}, u32[]{:S(2)}) copy-start(bf16[2,512,768]{2,1,0:T(8,128)(2,1)} %param.21) | copy-start | bytes 4718596
  4.3 96.6 %copy-start.26 = (bf16[2,512,768]{2,1,0:T(8,128)(2,1)S(1)}, bf16[2,512,768]{2,1,0:T(8,128)(2,1)}, u32[]{:S(2)}) copy-start(bf16[2,512,768]{2,1,0:T(8,128)(2,1)} %param.20) | copy-start | bytes 4718596
  119.8 3.1 copy-start.52
  147.0 4.6 copy-start
  147.0 4.6 copy-start.2
  147.0 4.7 copy-start.29
  151.7 3.5 copy-start.21
  173.5 11.3 %copy-start.41 = (f32[768]{0:T(1024)S(1)}, f32[768]{0:T(1024)}, u32[]{:S(2)}) copy-start(f32[768]{0:T(1024)} %get-tuple-element.248) | copy-start | bytes 9220
  173.5 11.3 %copy-start.47 = (f32[3072]{0:T(1024)S(1)}, f32[3072]{0:T(1024)}, u32[]{:S(2)}) copy-start(f32[3072]{0:T(1024)} %slice.73) | copy-start | bytes 36868
  173.5 11.3 %copy-start.48 = (f32[768]{0:T(1024)S(1)}, f32[768]{0:T(1024)}, u32[]{:S(2)}) copy-start(f32[768]{0:T(1024)} %get-tuple-element.247) | copy-start | bytes 9220
  184.8 37.1 %copy-start.49 = (f32[768]{0:T(1024)S(1)}, f32[768]{0:T(1024)}, u32[]{:S(2)}) copy-start(f32[768]{0:T(1024)} %get-tuple-element.246) | copy-start | bytes 9220
  221.9 10.0 %copy-start.54 = (bf16[1024,3072]{1,0:T(8,128)(2,1)}, bf16[1024,3072]{1,0:T(8,128)(2,1)S(1)}, u32[]{:S(2)}) copy-start(bf16[1024,3072]{1,0:T(8,128)(2,1)S(1)} %get-tuple-element.254) | copy-start | bytes 18874372
  232.5 3.2 copy-start.30
  232.5 3.1 copy-start.45
  233.3 6.5 %slice-start.2 = ((s8[4718592]{0:T(1024)(128)(4,1)}), s8[4194304]{0:T(1024)(128)(4,1)S(1)}, s32[]{:S(2)}) async-start(s8[4718592]{0:T(1024)(128)(4,1)} %bitcast.233), calls=%async_computation.2 | async-start | bytes 8388608
  235.6 4.2 slice-start.3
  237.8 24.4 %slice-start = ((s8[4718592]{0:T(1024)(128)(4,1)}), s8[4194304]{0:T(1024)(128)(4,1)S(1)}, s32[]{:S(2)}) async-start(s8[4718592]{0:T(1024)(128)(4,1)} %bitcast.230), calls=%async_computation | async-start | bytes 8388608
  239.8 22.4 %slice-start.1 = ((s8[4718592]{0:T(1024)(128)(4,1)}), s8[524288]{0:T(1024)(128)(4,1)S(1)}, s32[]{:S(2)}) async-start(s8[4718592]{0:T(1024)(128)(4,1)} %bitcast.230), calls=%async_computation.1 | async-start | bytes 1048576
  270.4 7.9 %copy-start.16 = (f32[1024,768]{1,0:T(8,128)}, f32[1024,768]{1,0:T(8,128)S(1)}, u32[]{:S(2)}) copy-start(f32[1024,768]{1,0:T(8,128)S(1)} %get-tuple-element.237) | copy-start | bytes 9437188
  270.4 7.9 %copy-start.22 = (bf16[96,8,2,512]{3,1,2,0:T(8,128)(2,1)S(1)}, bf16[96,8,2,512]{3,1,2,0:T(8,128)(2,1)}, u32[]{:S(2)}) copy-start(bf16[96,8,2,512]{3,1,2,0:T(8,128)(2,1)} %copy-done.21) | copy-start | bytes 4718596
  298.0 8.3 %copy-start.17 = (f32[1024,768]{1,0:T(8,128)S(1)}, f32[1024,768]{1,0:T(8,128)}, u32[]{:S(2)}) copy-start(f32[1024,768]{1,0:T(8,128)} %copy-done.16) | copy-start | bytes 9437188
  314.7 4.0 copy-start.1
  314.7 4.0 copy-start.3
  314.7 4.0 copy-start.33
  314.7 4.0 copy-start.53
  321.9 3.1 copy-start.8
  325.0 7.3 %copy-start.11 = (bf16[2,512,12,64]{1,3,2,0:T(8,128)(2,1)}, bf16[2,512,12,64]{1,3,2,0:T(8,128)(2,1)S(1)}, u32[]{:S(2)}) copy-start(bf16[2,512,12,64]{1,3,2,0:T(8,128)(2,1)S(1)} %bitcast_dynamic-update-slice_fusion.14) | copy-start | bytes 4718596 | tf_op jit(solution)/shard_map/while
  332.2 7.3 %copy-start.19 = (bf16[2,512,12,64]{1,3,2,0:T(8,128)(2,1)S(1)}, bf16[2,512,12,64]{1,3,2,0:T(8,128)(2,1)}, u32[]{:S(2)}) copy-start(bf16[2,512,12,64]{1,3,2,0:T(8,128)(2,1)} %get-tuple-element.412) | copy-start | bytes 4718596 | tf_op jit(solution)/shard_map/while
  347.0 3.1 copy-start.8
  350.1 7.3 %copy-start.11 = (bf16[2,512,12,64]{1,3,2,0:T(8,128)(2,1)}, bf16[2,512,12,64]{1,3,2,0:T(8,128)(2,1)S(1)}, u32[]{:S(2)}) copy-start(bf16[2,512,12,64]{1,3,2,0:T(8,128)(2,1)S(1)} %bitcast_dynamic-update-slice_fusion.14) | copy-start | bytes 4718596 | tf_op jit(solution)/shard_map/while
  357.3 7.3 %copy-start.19 = (bf16[2,512,12,64]{1,3,2,0:T(8,128)(2,1)S(1)}, bf16[2,512,12,64]{1,3,2,0:T(8,128)(2,1)}, u32[]{:S(2)}) copy-start(bf16[2,512,12,64]{1,3,2,0:T(8,128)(2,1)} %get-tuple-element.412) | copy-start | bytes 4718596 | tf_op jit(solution)/shard_map/while
  369.4 4.7 copy-start.12
  (36 other events, 60.8 us)
